TPU v7x, 512 devices: a whole 4x8x8 slice. The times are simulated.
512 devices in a mesh: sta: 8 (over z_hi, x), tm: 64 (over y, z_lo, core).
Axes of the slice: x: 4, y: 8, z: 8 (z_hi: 2, z_lo: 4; z = z_hi * 4 + z_lo), core: 2. Of those that a mesh axis runs over, the one named last changes fastest.
Arguments:
- record: bfloat16 [96, 49152], P('sta', 'tm')
- templates: bfloat16 [64, 96, 512], P('tm', 'sta'), may hold values from -6 to 6
- shifts: int32 [96], P('sta'), may hold values from 0 to 255, as said below
- live_mask: int32 [96], P('sta'), may hold values 0 or 1
- plan: int32 [64], replicated, may hold values from 0 to 63, each once
Outputs:
- stacks: float32 [64, 49152], P('sta', 'tm')
Inputs may be any that keep to these rules, and one draw needn't show every extreme that they name: `shifts`: some channel has the shift 256 - 1. `plan`: each bank slot appears once.
All inputs are finite; a program needn't handle non-finite values. No bound on the sum of `live_mask` on one device may be relied on, other than what follows from the above.
Results may differ from a plain program's by a relative error of at most 0.0003.
Values may be sent and summed in bfloat16 or wider, within the bound.
A program may use at most 64 MiB of HBM per device.

v0:
```python
import math
import jax
import jax.numpy as jnp
from jax import lax
from jax.sharding import PartitionSpec as P

CHANNELS = 96


def passed_along(shard, axis, by):
    count = lax.axis_size(axis)
    pairs = [(i, i + by) for i in range(count) if 0 <= i + by < count]
    return lax.ppermute(shard, axis, pairs)


def hankel_rows(signal, taps_len, span_len):
    length = signal.shape[0]
    copies = jnp.tile(signal, taps_len + 1)
    skewed = copies[: taps_len * (length + 1)].reshape(taps_len, length + 1)
    return skewed[:, :span_len]


def correlate(panels_in, aligned, live_vals, taps_len, span_len, group_cap):
    tmpl_rows, chan_count, _ = panels_in.shape
    group_size = math.gcd(chan_count, group_cap)
    overall = math.sqrt(taps_len / CHANNELS)
    norm_vals = jnp.sqrt(jnp.sum(jnp.square(panels_in.astype(jnp.float32)), axis=2) + 1e-06)
    weights = live_vals[None, :] * overall / norm_vals
    in_pos = lax.broadcasted_iota(jnp.int32, (span_len + taps_len, span_len), 0)
    out_pos = lax.broadcasted_iota(jnp.int32, (span_len + taps_len, span_len), 1)
    band_ones = ((in_pos >= out_pos) & (in_pos < out_pos + taps_len)).astype(jnp.float32)

    def add_group(group_idx, running):
        first_chan = group_idx * group_size
        panel_part = lax.dynamic_slice_in_dim(panels_in, first_chan, group_size, 1)
        window = lax.dynamic_slice_in_dim(aligned, first_chan, group_size, 0)
        stacked = jax.vmap(lambda signal_row: hankel_rows(signal_row, taps_len, span_len))(window)
        products = jnp.einsum(
            "rgl,glt->rgt", panel_part, stacked, preferred_element_type=jnp.float32
        )
        squares = jnp.square(window.astype(jnp.float32))
        energy = jnp.dot(squares, band_ones, precision=lax.Precision.HIGHEST)
        weighting = lax.dynamic_slice_in_dim(weights, first_chan, group_size, 1)
        scaled = products * weighting[:, :, None] * lax.rsqrt(energy + 1e-06)[None, :, :]
        return running + jnp.sum(scaled, axis=1)

    start_val = jnp.zeros((tmpl_rows, span_len), jnp.float32)
    return lax.fori_loop(0, chan_count // group_size, add_group, start_val)


def per_device(record, templates, shifts, live_mask, plan):
    taps_len = templates.shape[2]
    span_len = record.shape[1]
    live_vals = live_mask.astype(jnp.float32)
    rim_part = passed_along(record, "tm", -1)
    extended = jnp.concatenate([record, rim_part], axis=1)
    aligned = jax.vmap(
        lambda signal_row, lag_val: lax.dynamic_slice_in_dim(
            signal_row, lag_val, span_len + taps_len
        )
    )(extended, shifts)
    bank_all = lax.all_gather(templates, "tm", axis=0, tiled=True)
    ordered = jnp.take(bank_all, plan, axis=0)
    partial_value = correlate(ordered, aligned, live_vals, taps_len, span_len, 8)
    return lax.psum_scatter(partial_value, "sta", scatter_dimension=0, tiled=True)


def solution(mesh):
    placed = (P("sta", "tm"), P("tm", "sta", None), P("sta"), P("sta"), P())
    return jax.shard_map(
        per_device, mesh=mesh, in_specs=placed, out_specs=P("sta", "tm"), check_vma=False
    )
```

profile of v0, /device:TPU:8, one launch (start us, length us, event | category | flops | bytes accessed | tf_op | source)
XLA Modules:
  0.0 318.2 jit_solution(1732965342201204)
XLA Ops:
  6.5 7.3 %collective-permute-start = (bf16[12,768]{1,0:T(8,128)(2,1)}, bf16[12,768]{1,0:T(8,128)(2,1)S(1)}, u32[]{:S(2)}, u32[]{:S(2)}) collective-permute-start(bf16[12,768]{1,0:T(8,128)(2,1)} %param.7), channel_id=1, source_target_pairs={{1,0},{2,1},{3,2},{4,3},{5,4},{6,5},{7,6},{8,7},{9,8},{10,9},{11,1... | collective-permute-start | bytes 55304 | tf_op jit(solution)/shard_map/ppermute | solution.py:13
  15.9 73.3 %all_gather.3 = bf16[64,12,512]{2,1,0:T(8,128)(2,1)S(1)} all-gather(bf16[1,12,512]{2,1,0:T(8,128)(2,1)} %param.8), channel_id=1, replica_groups=mesh['sta'=8,'tm'=64] {'tm'}, dimensions={0}, use_global_device_ids=true | all-gather | bytes 798720 | tf_op jit(solution)/shard_map/all_gather | solution.py:62
  91.1 25.1 %while.15 = (s32[]{:T(128)}, bf16[12,1536]{1,0:T(8,128)(2,1)S(1)}, s32[12,2]{0,1:T(2,128)S(1)}, bf16[12,1280]{1,0:T(8,128)(2,1)S(1)}, s32[]{:T(128)}, /*index=5*/s32[]{:T(128)}) while((s32[]{:T(128)}, bf16[12,1536]{1,0:T(8,128)(2,1)S(1)}, s32[12,2]{0,1:T(2,128)S(1)}, bf16[12,1280]{1,0:T(8,128)(2,1)S(1)}, s32[]{:T(128)}, /*index=5*/s32[]{:T(128)}) %tuple.49), condition=%wide.while_cond, body=%wide.while_body.sunk | while | flops 2 | bytes 10361 | solution.py:58
  91.8 1.4 dynamic-slice.7
  93.9 1.4 dynamic-slice.7
  96.0 1.4 dynamic-slice.7
  98.1 1.4 dynamic-slice.7
  100.1 1.4 dynamic-slice.7
  102.2 1.4 dynamic-slice.7
  104.3 1.4 dynamic-slice.7
  106.4 1.4 dynamic-slice.7
  108.5 1.4 dynamic-slice.7
  116.2 98.8 %while.16 = (s32[]{:T(128)}, f32[64,768]{1,0:T(8,128)S(1)}, bf16[12,1280]{1,0:T(8,128)(2,1)S(1)}, bf16[64,12,512]{2,1,0:T(8,128)(2,1)S(1)}, f32[64,12]{0,1:T(8,1...) while((s32[]{:T(128)}, f32[64,768]{1,0:T(8,128)S(1)}, ...), condition=%wide.region_3.4_spmd.clone, body=%wide.region_1.3_spmd.clone.sunk | while | flops 253096960 | bytes 52031664 | solution.py:48
  116.6 2.0 copy.16
  118.6 4.0 %slice.49 = bf16[4,655872]{1,0:T(4,128)(2,1)} slice(bf16[4,656640]{1,0:T(4,128)(2,1)S(1)} %bitcast.25), slice={[0:4], [0:655872]} | slice | bytes 10493952 | tf_op jit(solution)/shard_map/while/body/eval_jaxpr/vmap()/slice | solution.py:19
  122.6 6.8 %reshape.53 = bf16[2623488]{0:T(1024)(128)(2,1)} reshape(bf16[4,655872]{1,0:T(4,128)(2,1)} %slice.49) | data formatting | bytes 10493952 | tf_op jit(solution)/shard_map/while
  129.5 14.9 %reshape.54 = bf16[4,512,1281]{2,1,0:T(8,128)(2,1)} reshape(bf16[2623488]{0:T(1024)(128)(2,1)} %reshape.53) | data formatting | bytes 10493952 | tf_op jit(solution)/shard_map/while/body/eval_jaxpr/vmap()/reshape | solution.py:19
  144.4 2.0 fusion.44
  146.5 2.6 fusion.45
  149.5 2.0 copy.16
  151.6 4.0 %slice.49 = bf16[4,655872]{1,0:T(4,128)(2,1)} slice(bf16[4,656640]{1,0:T(4,128)(2,1)S(1)} %bitcast.25), slice={[0:4], [0:655872]} | slice | bytes 10493952 | tf_op jit(solution)/shard_map/while/body/eval_jaxpr/vmap()/slice | solution.py:19
  155.6 6.8 %reshape.53 = bf16[2623488]{0:T(1024)(128)(2,1)} reshape(bf16[4,655872]{1,0:T(4,128)(2,1)} %slice.49) | data formatting | bytes 10493952 | tf_op jit(solution)/shard_map/while
  162.4 14.9 %reshape.54 = bf16[4,512,1281]{2,1,0:T(8,128)(2,1)} reshape(bf16[2623488]{0:T(1024)(128)(2,1)} %reshape.53) | data formatting | bytes 10493952 | tf_op jit(solution)/shard_map/while/body/eval_jaxpr/vmap()/reshape | solution.py:19
  177.3 2.0 fusion.44
  179.5 2.6 fusion.45
  182.5 2.0 copy.16
  184.5 4.0 %slice.49 = bf16[4,655872]{1,0:T(4,128)(2,1)} slice(bf16[4,656640]{1,0:T(4,128)(2,1)S(1)} %bitcast.25), slice={[0:4], [0:655872]} | slice | bytes 10493952 | tf_op jit(solution)/shard_map/while/body/eval_jaxpr/vmap()/slice | solution.py:19
  188.5 6.8 %reshape.53 = bf16[2623488]{0:T(1024)(128)(2,1)} reshape(bf16[4,655872]{1,0:T(4,128)(2,1)} %slice.49) | data formatting | bytes 10493952 | tf_op jit(solution)/shard_map/while
  195.4 14.9 %reshape.54 = bf16[4,512,1281]{2,1,0:T(8,128)(2,1)} reshape(bf16[2623488]{0:T(1024)(128)(2,1)} %reshape.53) | data formatting | bytes 10493952 | tf_op jit(solution)/shard_map/while/body/eval_jaxpr/vmap()/reshape | solution.py:19
  210.3 2.0 fusion.44
  212.4 2.6 fusion.45
  215.7 95.6 %reduce-scatter.2.cloned.1.call-done = f32[8,768]{1,0:T(8,128)} async-done(((f32[64,768]{1,0:T(8,128)}), f32[8,768]{1,0:T(8,128)}) %reduce-scatter.2.cloned.1.call-update) | async-done | bytes 24592 | tf_op jit(solution)/shard_map/reduce_scatter | solution.py:65
  (76 shorter events, 18.9 us)
Async XLA Ops:
  6.5 84.6 %copy-start.1 = (bf16[12,768]{1,0:T(8,128)(2,1)S(1)}, bf16[12,768]{1,0:T(8,128)(2,1)}, u32[]{:S(2)}) copy-start(bf16[12,768]{1,0:T(8,128)(2,1)} %param.7) | copy-start | bytes 55300
  6.5 304.8 %reduce-scatter.2.cloned.1.call-start = ((), (), s32[]{:S(2)}) async-start(), calls=%async_computation.1 | async-start | bytes 221184 | tf_op jit(solution)/shard_map/reduce_scatter | solution.py:65
  6.5 84.6 %collective-permute-start = (bf16[12,768]{1,0:T(8,128)(2,1)}, bf16[12,768]{1,0:T(8,128)(2,1)S(1)}, u32[]{:S(2)}, u32[]{:S(2)}) collective-permute-start(bf16[12,768]{1,0:T(8,128)(2,1)} %param.7), channel_id=1, source_target_pairs={{1,0},{2,1},{3,2},{4,3},{5,4},{6,5},{7,6},{8,7},{9,8},{10,9},{11,1... | collective-permute-start | bytes 55304 | tf_op jit(solution)/shard_map/ppermute | solution.py:13
  215.0 0.7 copy-start
Sparse Core Ops, SparseCore 0:
  215.9 95.4 reduce-scatter.1
where the time goes:
time: 319 us; the launch traced here: 318 us
  local copies, waits for them, and re-layouts  111 us (35%)
  waiting for transfers between devices  95.6 us (30%)
  blocking collectives  73.3 us (23%)
  matrix products  13.6 us (4%)
  between operations  13.5 us (4%)
  starting transfers between devices  7.34 us (2%)
  other arithmetic  3.33 us (1%)
    reduce_scatter x1, waiting for transfers between devices, per_device(): lax.psum_scatter(partial_value, 'sta', scatter_dimension=0, tiled=True)  95.6 us
    all_gather x1, blocking collectives, per_device(): bank_all = lax.all_gather(templates, 'tm', axis=0, tiled=True)  73.3 us
    reshape x3, local copies, waits for them, and re-layouts, hankel_rows(): skewed = copies[:taps_len * (length + 1)].reshape(taps_len, length + 1)  44.7 us
    while x9, local copies, waits for them, and re-layouts  27.6 us
    gather x48, local copies, waits for them, and re-layouts  24.8 us
    slice x3, local copies, waits for them, and re-layouts, hankel_rows(): skewed = copies[:taps_len * (length + 1)].reshape(taps_len, length + 1)  12 us
    dot_general x3, matrix products, add_group(): jnp.einsum('rgl,glt->rgt', panel_part, stacked, preferred_element_type=jn...  7.72 us
    ppermute x1, starting transfers between devices, passed_along(): return lax.ppermute(shard, axis, pairs)  7.34 us
  transfers between devices with their start and end apart: 2, of which 1 were waited for; matrix products, arithmetic and copies ran while one was open for 1% of the time, Pallas kernels for 0%

commit v1 on v0

--- a/solution.py
+++ b/solution.py
@@ -59,7 +59,9 @@
             signal_row, lag_val, span_len + taps_len
         )
     )(extended, shifts)
-    bank_all = lax.all_gather(templates, "tm", axis=0, tiled=True)
+    bank_all = jnp.concatenate(
+        lax.all_to_all(jnp.stack([templates] * lax.axis_size("tm")), "tm", 0, 0), axis=0
+    )
     ordered = jnp.take(bank_all, plan, axis=0)
     partial_value = correlate(ordered, aligned, live_vals, taps_len, span_len, 8)
     return lax.psum_scatter(partial_value, "sta", scatter_dimension=0, tiled=True)

time: 319 us -> 252 us (0.79)
  blocking collectives: 73.3 us -> 0 us
  starting transfers between devices: 7.34 us -> 15.6 us
  waiting for transfers between devices: 95.6 us -> 91.3 us
    all_gather x1 -> x0, blocking collectives: 73.3 us -> none  [per_device(): bank_all = lax.all_gather(templates, 'tm', axis=0, tiled=True)]
    all_to_all x0 -> x1, starting transfers between devices: none -> 8.33 us  [per_device(): lax.all_to_all(jnp.stack([templates] * lax.axis_size('tm')), 'tm', 0, 0)]
    reduce_scatter x1, waiting for transfers between devices: 95.6 us -> 91.2 us  [per_device(): lax.psum_scatter(partial_value, 'sta', scatter_dimension=0, tiled=True)]
  transfers between devices with their start and end apart: 2 -> 3, of which waited for: 1 -> 2; matrix products, arithmetic and copies ran while one was open for 1% -> 12% of each run, Pallas kernels for 0% -> 0%
where the time goes in v1:
time: 252 us; the launch traced here: 251 us
  local copies, waits for them, and re-layouts  112 us (44%)
  waiting for transfers between devices  91.3 us (36%)
  starting transfers between devices  15.6 us (6%)
  matrix products  13.6 us (5%)
  between operations  13.5 us (5%)
  other arithmetic  4.06 us (2%)
    reduce_scatter x1, waiting for transfers between devices, per_device(): lax.psum_scatter(partial_value, 'sta', scatter_dimension=0, tiled=True)  91.2 us
    reshape x3, local copies, waits for them, and re-layouts, hankel_rows(): skewed = copies[:taps_len * (length + 1)].reshape(taps_len, length + 1)  44.7 us
    while x9, local copies, waits for them, and re-layouts  27.6 us
    gather x48, local copies, waits for them, and re-layouts  24 us
    slice x3, local copies, waits for them, and re-layouts, hankel_rows(): skewed = copies[:taps_len * (length + 1)].reshape(taps_len, length + 1)  12.1 us
    all_to_all x1, starting transfers between devices, per_device(): lax.all_to_all(jnp.stack([templates] * lax.axis_size('tm')), 'tm', 0, 0)  8.33 us
    dot_general x3, matrix products, add_group(): jnp.einsum('rgl,glt->rgt', panel_part, stacked, preferred_element_type=jn...  7.72 us
    ppermute x1, starting transfers between devices, passed_along(): return lax.ppermute(shard, axis, pairs)  7.21 us
  transfers between devices with their start and end apart: 3, of which 2 were waited for; matrix products, arithmetic and copies ran while one was open for 12% of the time, Pallas kernels for 0%

profile of v1, /device:TPU:8, one launch (start us, length us, event | category | flops | bytes accessed | tf_op | source)
XLA Modules:
  0.0 250.8 jit_solution(2806785707973988296)
XLA Ops:
  6.5 7.2 %collective-permute-start = (bf16[12,768]{1,0:T(8,128)(2,1)}, bf16[12,768]{1,0:T(8,128)(2,1)S(1)}, u32[]{:S(2)}, u32[]{:S(2)}) collective-permute-start(bf16[12,768]{1,0:T(8,128)(2,1)} %param.7), channel_id=1, source_target_pairs={{1,0},{2,1},{3,2},{4,3},{5,4},{6,5},{7,6},{8,7},{9,8},{10,9},{11,1... | collective-permute-start | bytes 55304 | tf_op jit(solution)/shard_map/ppermute | solution.py:13
  13.8 1.8 stack.2
  15.6 8.3 %all-to-all-start = ((bf16[64,1,12,512]{3,2,1,0:T(8,128)(2,1)}), bf16[64,1,12,512]{3,2,1,0:T(8,128)(2,1)S(1)}, u32[]{:S(2)}, u32[]{:S(2)}) async-start(bf16[64,1,12,512]{3,2,1,0:T(8,128)(2,1)} %stack.2), calls=%async_computation | async-start | bytes 2097152 | tf_op jit(solution)/shard_map/all_to_all | solution.py:63
  27.4 24.3 %while.15 = (s32[]{:T(128)}, bf16[12,1536]{1,0:T(8,128)(2,1)S(1)}, s32[12,2]{0,1:T(2,128)S(1)}, bf16[12,1280]{1,0:T(8,128)(2,1)S(1)}, s32[]{:T(128)}, /*index=5*/s32[]{:T(128)}) while((s32[]{:T(128)}, bf16[12,1536]{1,0:T(8,128)(2,1)S(1)}, s32[12,2]{0,1:T(2,128)S(1)}, bf16[12,1280]{1,0:T(8,128)(2,1)S(1)}, s32[]{:T(128)}, /*index=5*/s32[]{:T(128)}) %tuple.49), condition=%wide.while_cond, body=%wide.while_body.sunk | while | flops 2 | bytes 10361 | solution.py:58
  28.1 1.3 dynamic-slice.7
  30.1 1.3 dynamic-slice.7
  32.1 1.3 dynamic-slice.7
  34.1 1.3 dynamic-slice.7
  36.2 1.3 dynamic-slice.7
  38.2 1.3 dynamic-slice.7
  40.2 1.3 dynamic-slice.7
  48.3 1.3 dynamic-slice.7
  53.0 99.0 %while.16 = (s32[]{:T(128)}, f32[64,768]{1,0:T(8,128)S(1)}, bf16[12,1280]{1,0:T(8,128)(2,1)S(1)}, bf16[64,12,512]{2,1,0:T(8,128)(2,1)S(1)}, f32[64,12]{0,1:T(8,1...) while((s32[]{:T(128)}, f32[64,768]{1,0:T(8,128)S(1)}, ...), condition=%wide.region_3.4_spmd.clone, body=%wide.region_1.3_spmd.clone.sunk | while | flops 253096960 | bytes 52031664 | solution.py:48
  53.4 2.0 copy.16
  55.4 4.0 %slice.49 = bf16[4,655872]{1,0:T(4,128)(2,1)} slice(bf16[4,656640]{1,0:T(4,128)(2,1)S(1)} %bitcast.27), slice={[0:4], [0:655872]} | slice | bytes 10493952 | tf_op jit(solution)/shard_map/while/body/eval_jaxpr/vmap()/slice | solution.py:19
  59.5 6.8 %reshape.60 = bf16[2623488]{0:T(1024)(128)(2,1)} reshape(bf16[4,655872]{1,0:T(4,128)(2,1)} %slice.49) | data formatting | bytes 10493952 | tf_op jit(solution)/shard_map/while
  66.3 14.9 %reshape.61 = bf16[4,512,1281]{2,1,0:T(8,128)(2,1)} reshape(bf16[2623488]{0:T(1024)(128)(2,1)} %reshape.60) | data formatting | bytes 10493952 | tf_op jit(solution)/shard_map/while/body/eval_jaxpr/vmap()/reshape | solution.py:19
  81.2 2.0 fusion.44
  83.4 2.6 %fusion.45 = f32[64,768]{1,0:T(8,128)S(1)} fusion(bf16[4,512,1281]{2,1,0:T(8,128)(2,1)} %reshape.61, f32[4,768]{1,0:T(4,128)S(1)} %fusion.44, f32[64,4]{0,1:T(4,128)S(1)} %constant_dynamic-slice_fusion.10, bf16[64,4,512]{2,1,0:T(4,128)(2,1)S(1)} %constant_dynamic-slice_fusion.11), kind=kOutput, calls=%fused_computation.15.clone.1 | convolution fusion | flops 201867264 | bytes 3617792 | tf_op jit(solution)/shard_map/while/body/eval_jaxpr/rgl,glt->rgt/dot_general | solution.py:38
  86.4 2.0 copy.16
  88.4 4.0 %slice.49 = bf16[4,655872]{1,0:T(4,128)(2,1)} slice(bf16[4,656640]{1,0:T(4,128)(2,1)S(1)} %bitcast.27), slice={[0:4], [0:655872]} | slice | bytes 10493952 | tf_op jit(solution)/shard_map/while/body/eval_jaxpr/vmap()/slice | solution.py:19
  92.5 6.8 %reshape.60 = bf16[2623488]{0:T(1024)(128)(2,1)} reshape(bf16[4,655872]{1,0:T(4,128)(2,1)} %slice.49) | data formatting | bytes 10493952 | tf_op jit(solution)/shard_map/while
  99.3 14.9 %reshape.61 = bf16[4,512,1281]{2,1,0:T(8,128)(2,1)} reshape(bf16[2623488]{0:T(1024)(128)(2,1)} %reshape.60) | data formatting | bytes 10493952 | tf_op jit(solution)/shard_map/while/body/eval_jaxpr/vmap()/reshape | solution.py:19
  114.2 2.0 fusion.44
  116.4 2.6 %fusion.45 = f32[64,768]{1,0:T(8,128)S(1)} fusion(bf16[4,512,1281]{2,1,0:T(8,128)(2,1)} %reshape.61, f32[4,768]{1,0:T(4,128)S(1)} %fusion.44, f32[64,4]{0,1:T(4,128)S(1)} %constant_dynamic-slice_fusion.10, bf16[64,4,512]{2,1,0:T(4,128)(2,1)S(1)} %constant_dynamic-slice_fusion.11), kind=kOutput, calls=%fused_computation.15.clone.1 | convolution fusion | flops 201867264 | bytes 3617792 | tf_op jit(solution)/shard_map/while/body/eval_jaxpr/rgl,glt->rgt/dot_general | solution.py:38
  119.4 2.0 copy.16
  121.4 4.0 %slice.49 = bf16[4,655872]{1,0:T(4,128)(2,1)} slice(bf16[4,656640]{1,0:T(4,128)(2,1)S(1)} %bitcast.27), slice={[0:4], [0:655872]} | slice | bytes 10493952 | tf_op jit(solution)/shard_map/while/body/eval_jaxpr/vmap()/slice | solution.py:19
  125.5 6.8 %reshape.60 = bf16[2623488]{0:T(1024)(128)(2,1)} reshape(bf16[4,655872]{1,0:T(4,128)(2,1)} %slice.49) | data formatting | bytes 10493952 | tf_op jit(solution)/shard_map/while
  132.3 14.9 %reshape.61 = bf16[4,512,1281]{2,1,0:T(8,128)(2,1)} reshape(bf16[2623488]{0:T(1024)(128)(2,1)} %reshape.60) | data formatting | bytes 10493952 | tf_op jit(solution)/shard_map/while/body/eval_jaxpr/vmap()/reshape | solution.py:19
  147.2 2.0 fusion.44
  149.4 2.6 %fusion.45 = f32[64,768]{1,0:T(8,128)S(1)} fusion(bf16[4,512,1281]{2,1,0:T(8,128)(2,1)} %reshape.61, f32[4,768]{1,0:T(4,128)S(1)} %fusion.44, f32[64,4]{0,1:T(4,128)S(1)} %constant_dynamic-slice_fusion.10, bf16[64,4,512]{2,1,0:T(4,128)(2,1)S(1)} %constant_dynamic-slice_fusion.11), kind=kOutput, calls=%fused_computation.15.clone.1 | convolution fusion | flops 201867264 | bytes 3617792 | tf_op jit(solution)/shard_map/while/body/eval_jaxpr/rgl,glt->rgt/dot_general | solution.py:38
  152.7 91.2 %reduce-scatter.2.cloned.1.call-done = f32[8,768]{1,0:T(8,128)} async-done(((f32[64,768]{1,0:T(8,128)}), f32[8,768]{1,0:T(8,128)}) %reduce-scatter.2.cloned.1.call-update) | async-done | bytes 24592 | tf_op jit(solution)/shard_map/reduce_scatter | solution.py:67
  (76 shorter events, 20.9 us)
Async XLA Ops:
  6.5 20.1 %collective-permute-start = (bf16[12,768]{1,0:T(8,128)(2,1)}, bf16[12,768]{1,0:T(8,128)(2,1)S(1)}, u32[]{:S(2)}, u32[]{:S(2)}) collective-permute-start(bf16[12,768]{1,0:T(8,128)(2,1)} %param.7), channel_id=1, source_target_pairs={{1,0},{2,1},{3,2},{4,3},{5,4},{6,5},{7,6},{8,7},{9,8},{10,9},{11,1... | collective-permute-start | bytes 55304 | tf_op jit(solution)/shard_map/ppermute | solution.py:13
  15.6 36.2 %all-to-all-start = ((bf16[64,1,12,512]{3,2,1,0:T(8,128)(2,1)}), bf16[64,1,12,512]{3,2,1,0:T(8,128)(2,1)S(1)}, u32[]{:S(2)}, u32[]{:S(2)}) async-start(bf16[64,1,12,512]{3,2,1,0:T(8,128)(2,1)} %stack.2), calls=%async_computation | async-start | bytes 2097152 | tf_op jit(solution)/shard_map/all_to_all | solution.py:63
  23.9 220.0 %reduce-scatter.2.cloned.1.call-start = ((), (), s32[]{:S(2)}) async-start(), calls=%async_computation.2 | async-start | bytes 221184 | tf_op jit(solution)/shard_map/reduce_scatter | solution.py:67
  152.0 0.7 copy-start
Sparse Core Ops, SparseCore 0:
  152.8 91.0 reduce-scatter.1
